TPU v7x, 256 devices: a whole 4x4x8 slice. The times are simulated.
256 devices in a mesh: vertex: 16 (over z, core), tm: 16 (over y, x).
Axes of the slice: x: 4, y: 4, z: 8, core: 2. Of those that a mesh axis runs over, the one named last changes fastest.
Arguments:
- features: bfloat16 [16, 16384, 512], P('tm', 'vertex'), may hold values from -6 to 6
- tile_coord: int32 [16, 2048, 2], P('tm', 'vertex'), may hold values from 0 to 127, as said below
- tile_count: int32 [16, 16], P('tm', 'vertex'), may hold values from 1 to 128, as said below
- tile_values: bfloat16 [16, 2048, 128, 128], P('tm', 'vertex'), may hold values from -0.125 to 0.125
- w_agg: bfloat16 [512, 512], replicated, may hold values from -0.25 to 0.25
- w_root: bfloat16 [512, 512], replicated, may hold values from -0.25 to 0.25
- time_embed: bfloat16 [16, 512], replicated, may hold values from -6 to 6
- gain_first: bfloat16 [512], replicated, may hold values from 0.25 to 1.75
- w_qkv: bfloat16 [512, 1536], replicated, may hold values from -12 to 12
- w_out: bfloat16 [512, 512], replicated, may hold values from -0.25 to 0.25
- gain_second: bfloat16 [512], replicated, may hold values from 0.25 to 1.75
- w_up: bfloat16 [512, 1024], replicated, may hold values from -0.25 to 0.25
- w_down: bfloat16 [1024, 512], replicated, may hold values from -0.1875 to 0.1875
Outputs:
- layer_out: bfloat16 [16, 16384, 512], P(None, ('vertex', 'tm'))
Inputs may be any that keep to these rules, and one draw needn't show every extreme that they name: `tile_coord`: entry 0 of a slot is a row block 0 to 7 of the device's own vertices, entry 1 a column block 0 to 127; no pair repeats among one device's 128 slots, live or not. `tile_count`: live slots are the first ones of a device; in every snapshot some device has all 128 slots live.
All inputs are finite; a program needn't handle non-finite values.
Results may differ from a plain program's by a relative error of at most 0.006.
Values may be sent and summed in bfloat16 or wider, within the bound.
No kernel may reach another device: no remote copies, remote signals or barrier semaphores. Data moves between devices by JAX's collectives and lax.ppermute only.
A program may use at most 192 MiB of HBM per device.

v0:
```python
import math
import jax
import jax.numpy as jnp
from jax import lax
from jax.sharding import PartitionSpec as P

HEADS = 8


def norm_rows(values, gain):
    scale = lax.rsqrt(jnp.mean(values * values, axis=-1, keepdims=True) + 1e-06)
    return values * scale * gain.astype(jnp.float32)


def project(left, right):
    return jnp.einsum("sid,de->sie", left, right, preferred_element_type=jnp.float32)


def temporal(graph_rows, time_embed, gain_first, w_qkv, w_out, gain_second, w_up, w_down):
    snap_count, item_count, width = graph_rows.shape
    head_size = width // HEADS
    mixed = graph_rows.astype(jnp.float32) + time_embed.astype(jnp.float32)[:, None, :]
    normed = norm_rows(mixed, gain_first).astype(jnp.bfloat16)
    qkv = project(normed, w_qkv).astype(jnp.bfloat16)
    query = qkv[..., :width].reshape(snap_count, item_count, HEADS, head_size)
    key_rows = qkv[..., width : 2 * width].reshape(snap_count, item_count, HEADS, head_size)
    value_rows = qkv[..., 2 * width :].reshape(snap_count, item_count, HEADS, head_size)
    scores = jnp.einsum(
        "sihd,tihd->ihst", query, key_rows, preferred_element_type=jnp.float32
    ) / math.sqrt(head_size)
    causal = jnp.arange(snap_count)[:, None] >= jnp.arange(snap_count)[None, :]
    scores = jnp.where(causal, scores, -1e30)
    largest = jnp.max(scores, axis=-1, keepdims=True)
    expo = jnp.where(causal, jnp.exp(scores - largest), 0.0)
    weights_soft = (expo / jnp.sum(expo, axis=-1, keepdims=True)).astype(jnp.bfloat16)
    context = jnp.einsum(
        "ihst,tihd->sihd", weights_soft, value_rows, preferred_element_type=jnp.float32
    )
    context = context.astype(jnp.bfloat16).reshape(snap_count, item_count, width)
    residual = mixed + project(context, w_out)
    normed_two = norm_rows(residual, gain_second).astype(jnp.bfloat16)
    hidden = jax.nn.gelu(project(normed_two, w_up)).astype(jnp.bfloat16)
    return (residual + project(hidden, w_down)).astype(jnp.bfloat16)


def per_device(
    features,
    tile_coord,
    tile_count,
    tile_values,
    w_agg,
    w_root,
    time_embed,
    gain_first,
    w_qkv,
    w_out,
    gain_second,
    w_up,
    w_down,
):
    own_rows = features[0]
    tile_pairs = tile_coord[0]
    live_count = tile_count[0, 0]
    tile_block = tile_values[0]
    local_vertices, width = own_rows.shape
    tile_size = tile_block.shape[1]
    row_blocks = local_vertices // tile_size
    slot_count = tile_block.shape[0]
    alive = jnp.arange(slot_count) < live_count
    gathered = lax.all_gather(own_rows, "vertex", axis=0, tiled=True)
    blocks = gathered.reshape(-1, tile_size, width)
    chosen = blocks[tile_pairs[:, 1]]
    products = jnp.einsum("tij,tjd->tid", tile_block, chosen, preferred_element_type=jnp.float32)
    products = jnp.where(alive[:, None, None], products, 0.0)
    summed = jax.ops.segment_sum(products, tile_pairs[:, 0], num_segments=row_blocks)
    summed = summed.reshape(local_vertices, width)
    neighbor_sum = summed.astype(jnp.bfloat16)
    combined = jnp.dot(neighbor_sum, w_agg, preferred_element_type=jnp.float32)
    combined = combined + jnp.dot(own_rows, w_root, preferred_element_type=jnp.float32)
    graph_rows = jax.nn.gelu(combined).astype(jnp.bfloat16)
    tm_count = lax.axis_size("tm")
    sectioned = graph_rows.reshape(1, tm_count, local_vertices // tm_count, width)
    mixed_out = temporal(
        lax.all_to_all(sectioned, "tm", split_axis=1, concat_axis=0, tiled=True)[:, 0],
        time_embed,
        gain_first,
        w_qkv,
        w_out,
        gain_second,
        w_up,
        w_down,
    )
    result = mixed_out[:, None]
    return result[:, 0]


def solution(mesh):
    return jax.shard_map(
        per_device,
        mesh=mesh,
        in_specs=(
            P("tm", "vertex", None),
            P("tm", "vertex", None),
            P("tm", "vertex"),
            P("tm", "vertex", None, None),
            P(),
            P(),
            P(),
            P(),
            P(),
            P(),
            P(),
            P(),
            P(),
        ),
        out_specs=P(None, ("vertex", "tm"), None),
        check_vma=False,
    )
```

profile of v0, /device:TPU:1, one launch (start us, length us, event | category | flops | bytes accessed | tf_op | source)
XLA Modules:
  0.0 339.0 jit_solution(8120423000765595668)
XLA Ops:
  6.5 0.0 copy-start
  6.5 0.0 all-gather.3.cloned.1.call-start
  6.5 0.7 all-gather.3.cloned.1.call-update
  7.9 0.8 fusion.53
  8.7 100.1 %all-gather.3.cloned.1.call-done = bf16[1,16384,512]{2,1,0:T(8,128)(2,1)} async-done(((bf16[1,1024,512]{2,1,0:T(8,128)(2,1)}), bf16[1,16384,512]{2,1,0:T(8,128)(2,1)}) %all-gather.3.cloned.1.call-update) | async-done | bytes 16777232 | tf_op jit(solution)/shard_map/all_gather | solution.py:70
  108.7 14.1 %gather_fusion = bf16[128,128,512]{2,1,0:T(8,128)(2,1)} fusion(bf16[128,128,512]{2,1,0:T(8,128)(2,1)} %bitcast.55, s32[1024]{0:T(1024)S(1)} %pad_clamp_fusion), kind=kCustom, calls=%fused_computation | custom fusion | bytes 33554944 | tf_op jit(solution)/shard_map/gather | solution.py:72
  122.8 22.4 %select_bitcast_fusion = f32[128,128,512]{1,2,0:T(8,128)} fusion(pred[128]{0:T(512)(128)(4,1)S(1)} %iota_compare_fusion.1, bf16[128,128,512]{2,1,0:T(8,128)(2,1)} %gather_fusion, bf16[1,128,128,128]{3,2,1,0:T(8,128)(2,1)} %param.16), kind=kOutput, calls=%fused_computation.3 | convolution fusion | flops 2155872256 | bytes 54526080 | tf_op jit(solution)/shard_map/tij,tjd->tid/dot_general | solution.py:73
  145.2 33.5 %copy.36 = f32[128,128,512]{2,1,0:T(8,128)} copy(f32[128,128,512]{1,2,0:T(8,128)} %select_bitcast_fusion) | data formatting | bytes 67108864 | tf_op jit(solution)/shard_map/jit(_where)/select_n | solution.py:74
  178.7 1.6 broadcast_in_dim.40
  180.3 69.9 %scatter_fusion = f32[8,128,512]{2,1,0:T(8,128)} fusion(f32[8,128,512]{2,1,0:T(8,128)} %broadcast_in_dim.40, s32[128]{0:T(128)S(1)} %get-tuple-element.9, f32[128,128,512]{2,1,0:T(8,128)} %copy.36), kind=kCustom, calls=%fused_computation.1 | custom fusion | flops 8388608 | bytes 100663808 | tf_op jit(solution)/shard_map/scatter-add | solution.py:75
  250.2 0.0 copy-start.2
  250.2 1.8 convert_element_type.48
  252.0 0.0 copy-start.1
  252.0 0.0 copy-start.6
  252.0 0.0 copy-done.2
  252.0 0.7 fusion.62
  252.7 0.5 copy-done.1
  253.2 0.1 copy-done.6
  253.3 2.1 fusion.17
  255.4 0.0 copy-start.3
  255.5 0.0 copy-start.4
  255.5 0.0 copy-start.5
  255.5 7.0 %all-to-all-start = ((bf16[1,16,64,512]{3,2,0,1:T(8,128)(2,1)}), bf16[1,16,64,512]{3,2,0,1:T(8,128)(2,1)S(1)}, u32[]{:S(2)}, u32[]{:S(2)}) async-start(bf16[1,16,64,512]{3,2,0,1:T(8,128)(2,1)} %bitcast.57), calls=%async_computation | async-start | bytes 2097152 | tf_op jit(solution)/shard_map/all_to_all | solution.py:84
  262.4 0.0 copy-done.3
  262.5 0.0 copy-done.4
  262.5 0.0 copy-done.5
  262.5 16.4 %all-to-all-done = bf16[1,16,64,512]{3,2,0,1:T(8,128)(2,1)S(1)} async-done(((bf16[1,16,64,512]{3,2,0,1:T(8,128)(2,1)}), bf16[1,16,64,512]{3,2,0,1:T(8,128)(2,1)S(1)}, u32[]{:S(2)}, u32[]{:S(2)}) %all-to-all-start) | async-done | bytes 1048608 | tf_op jit(solution)/shard_map/all_to_all | solution.py:84
  278.9 0.3 fusion.21
  279.3 0.0 copy-done
  279.3 1.9 convolution_convert_fusion
  281.1 1.8 fusion.60
  282.9 3.9 %reshape.54 = bf16[16,64,8,64]{3,2,1,0:T(8,128)(2,1)} reshape(bf16[16,64,512]{2,1,0:T(8,128)(2,1)} %get-tuple-element.7) | data formatting | bytes 2097152 | tf_op jit(solution)/shard_map/reshape | solution.py:25
  286.8 3.9 %reshape.55 = bf16[16,64,8,64]{3,2,1,0:T(8,128)(2,1)} reshape(bf16[16,64,512]{2,1,0:T(8,128)(2,1)} %get-tuple-element.6) | data formatting | bytes 2097152 | tf_op jit(solution)/shard_map/reshape | solution.py:26
  290.7 6.7 %fusion.26 = f32[64,8,16,16]{2,3,1,0:T(8,128)} fusion(bf16[16,64,8,64]{3,2,1,0:T(8,128)(2,1)} %reshape.55, bf16[16,64,8,64]{3,2,1,0:T(8,128)(2,1)} %reshape.54), kind=kOutput, calls=%fused_computation.33 | convolution fusion | flops 16777216 | bytes 2621440 | tf_op jit(solution)/shard_map/sihd,tihd->ihst/dot_general | solution.py:28
  297.4 4.7 %copy.41 = f32[64,8,16,16]{0,3,2,1:T(8,128)} copy(f32[64,8,16,16]{2,3,1,0:T(8,128)} %fusion.26) | data formatting | bytes 1048576 | tf_op jit(solution)/shard_map/sihd,tihd->ihst/dot_general | solution.py:28
  302.1 2.6 fusion.61
  304.7 0.1 divide_convert_fusion
  304.9 3.9 %copy.43 = bf16[64,8,16,16]{3,2,1,0:T(8,128)(2,1)} copy(bf16[64,8,16,16]{0,3,2,1:T(8,128)(2,1)S(1)} %divide_convert_fusion) | data formatting | bytes 524288 | tf_op jit(solution)/shard_map/convert_element_type | solution.py:35
  308.8 3.9 %reshape.53 = bf16[16,64,8,64]{3,2,1,0:T(8,128)(2,1)} reshape(bf16[16,64,512]{2,1,0:T(8,128)(2,1)} %get-tuple-element.5) | data formatting | bytes 2097152 | tf_op jit(solution)/shard_map/reshape | solution.py:27
  312.7 3.7 %convert_bitcast_fusion = bf16[16,64,8,64]{3,0,2,1:T(8,128)(2,1)S(1)} fusion(bf16[64,8,16,16]{3,2,1,0:T(8,128)(2,1)} %copy.43, bf16[16,64,8,64]{3,2,1,0:T(8,128)(2,1)} %reshape.53), kind=kOutput, calls=%fused_computation.39 | convolution fusion | flops 17301504 | bytes 2359296 | tf_op jit(solution)/shard_map/ihst,tihd->sihd/dot_general | solution.py:36
  316.4 1.9 copy.44
  318.3 4.0 %reshape.56 = bf16[16,64,512]{2,1,0:T(8,128)(2,1)} reshape(bf16[16,64,8,64]{3,2,1,0:T(8,128)(2,1)} %copy.44) | data formatting | bytes 2097152 | tf_op jit(solution)/shard_map/reshape | solution.py:39
  322.4 3.5 %multiply_reduce_fusion = (f32[16,64]{1,0:T(8,128)S(1)}, f32[16,64,512]{2,1,0:T(8,128)}) fusion(bf16[16,64,512]{2,1,0:T(8,128)(2,1)} %reshape.56, bf16[512,512]{1,0:T(8,128)(2,1)} %param.22, f32[16,512]{1,0:T(8,128)S(1)} %convert_element_type.53, bf16[1,16,64,512]{3,2,0,1:T(8,128)(2,1)S(1)} %all-to-all-done), kind=kOutput, calls=%fused_computation.38 | convolution fusion | flops 539491328 | bytes 4755456 | tf_op jit(solution)/shard_map/sid,de->sie/dot_general | solution.py:16
  325.8 6.3 %add_convert_fusion = bf16[16,64,512]{2,1,0:T(8,128)(2,1)} fusion(f32[16,64,512]{2,1,0:T(8,128)} %get-tuple-element.13, bf16[1024,512]{1,0:T(8,128)(2,1)} %param.25, bf16[512,1024]{1,0:T(8,128)(2,1)} %param.24, f32[512]{0:T(512)S(1)} %convert_element_type.60, f32[16,64]{1,0:T(8,128)S(1)} %add_rsqrt_fusion), kind=kOutput, calls=%fused_computation.36 | convolution fusion | flops 2159542272 | bytes 5249024 | tf_op jit(solution)/shard_map/sid,de->sie/dot_general | solution.py:16
  (8 shorter events, 0.0 us)
Async XLA Ops:
  6.5 272.7 %copy-start = (bf16[512,1536]{1,0:T(8,128)(2,1)S(1)}, bf16[512,1536]{1,0:T(8,128)(2,1)}, u32[]{:S(2)}) copy-start(bf16[512,1536]{1,0:T(8,128)(2,1)} %param.21) | copy-start | bytes 4718596
  6.5 102.2 %all-gather.3.cloned.1.call-start = ((), (), s32[]{:S(2)}) async-start(), calls=%async_computation.1 | async-start | bytes 17825792 | tf_op jit(solution)/shard_map/all_gather | solution.py:70
  250.2 1.8 copy-start.2
  252.0 1.2 copy-start.1
  252.0 1.3 copy-start.6
  255.4 7.0 %copy-start.3 = (bf16[16,512]{1,0:T(8,128)(2,1)S(1)}, bf16[16,512]{1,0:T(8,128)(2,1)}, u32[]{:S(2)}) copy-start(bf16[16,512]{1,0:T(8,128)(2,1)} %param.19) | copy-start | bytes 49156
  255.5 7.0 %copy-start.4 = (bf16[512]{0:T(512)(128)(2,1)S(1)}, bf16[512]{0:T(512)(128)(2,1)}, u32[]{:S(2)}) copy-start(bf16[512]{0:T(512)(128)(2,1)} %param.20) | copy-start | bytes 3076
  255.5 7.0 %copy-start.5 = (bf16[512]{0:T(512)(128)(2,1)S(1)}, bf16[512]{0:T(512)(128)(2,1)}, u32[]{:S(2)}) copy-start(bf16[512]{0:T(512)(128)(2,1)} %param.23) | copy-start | bytes 3076
  255.5 23.5 %all-to-all-start = ((bf16[1,16,64,512]{3,2,0,1:T(8,128)(2,1)}), bf16[1,16,64,512]{3,2,0,1:T(8,128)(2,1)S(1)}, u32[]{:S(2)}, u32[]{:S(2)}) async-start(bf16[1,16,64,512]{3,2,0,1:T(8,128)(2,1)} %bitcast.57), calls=%async_computation | async-start | bytes 2097152 | tf_op jit(solution)/shard_map/all_to_all | solution.py:84
Sparse Core Ops, SparseCore 0:
  9.2 99.5 all-gather.2
where the time goes:
time: 340 us; the launch traced here: 339 us
  waiting for transfers between devices  117 us (34%)
  local copies, waits for them, and re-layouts  77.8 us (23%)
  other arithmetic  75.6 us (22%)
  matrix products  47.3 us (14%)
  between operations  14.2 us (4%)
  starting transfers between devices  6.97 us (2%)
    all_gather x1, waiting for transfers between devices, per_device(): gathered = lax.all_gather(own_rows, 'vertex', axis=0, tiled=True)  100 us
    scatter-add x1, other arithmetic, per_device(): jax.ops.segment_sum(products, tile_pairs[:, 0], num_segments=row_blocks)  69.9 us
    select_n x1, local copies, waits for them, and re-layouts, per_device(): products = jnp.where(alive[:, None, None], products, 0.0)  33.5 us
    dot_general x1, matrix products, per_device(): jnp.einsum('tij,tjd->tid', tile_block, chosen, preferred_element_type=jnp...  22.4 us
    all_to_all x1, waiting for transfers between devices, per_device(): lax.all_to_all(sectioned, 'tm', split_axis=1, concat_axis=0, tiled=True)  16.4 us
    gather x1, local copies, waits for them, and re-layouts, per_device(): chosen = blocks[tile_pairs[:, 1]]  14.1 us
    dot_general x3, matrix products, project(): jnp.einsum('sid,de->sie', left, right, preferred_element_type=jnp.float32)  11.6 us
    all_to_all x1, starting transfers between devices, per_device(): lax.all_to_all(sectioned, 'tm', split_axis=1, concat_axis=0, tiled=True)  6.97 us
  transfers between devices with their start and end apart: 2, of which 2 were waited for; matrix products, arithmetic and copies ran while one was open for 0% of the time, Pallas kernels for 0%

commit v1 on v0

--- a/solution.py
+++ b/solution.py
@@ -5,6 +5,11 @@
 from jax.sharding import PartitionSpec as P
 
 HEADS = 8
+
+
+def tiled_gather(x, axis, dim):
+    copies = jnp.concatenate([x] * lax.axis_size(axis), axis=dim)
+    return lax.all_to_all(copies, axis, dim, dim, tiled=True)
 
 
 def norm_rows(values, gain):
@@ -67,7 +72,7 @@
     row_blocks = local_vertices // tile_size
     slot_count = tile_block.shape[0]
     alive = jnp.arange(slot_count) < live_count
-    gathered = lax.all_gather(own_rows, "vertex", axis=0, tiled=True)
+    gathered = tiled_gather(own_rows, "vertex", 0)
     blocks = gathered.reshape(-1, tile_size, width)
     chosen = blocks[tile_pairs[:, 1]]
     products = jnp.einsum("tij,tjd->tid", tile_block, chosen, preferred_element_type=jnp.float32)

time: 340 us -> 608 us (1.79)
  waiting for transfers between devices: 117 us -> 378 us
  between operations: 14.2 us -> 0.99 us
  starting transfers between devices: 6.97 us -> 17.2 us
  local copies, waits for them, and re-layouts: 77.8 us -> 86.6 us
    all_to_all x0 -> x1, waiting for transfers between devices: none -> 362 us  [tiled_gather(): return lax.all_to_all(copies, axis, dim, dim, tiled=True)]
    all_gather x1 -> x0, waiting for transfers between devices: 100 us -> none  [per_device(): gathered = lax.all_gather(own_rows, 'vertex', axis=0, tiled=True)]
    all_to_all x0 -> x1, starting transfers between devices: none -> 10.1 us  [tiled_gather(): return lax.all_to_all(copies, axis, dim, dim, tiled=True)]
    unnamed x14 -> x35, local copies, waits for them, and re-layouts: 0.65 us -> 9.39 us
where the time goes in v1:
time: 608 us; the launch traced here: 605 us
  waiting for transfers between devices  378 us (62%)
  local copies, waits for them, and re-layouts  86.6 us (14%)
  other arithmetic  74.8 us (12%)
  matrix products  47.2 us (8%)
  starting transfers between devices  17.2 us (3%)
    all_to_all x1, waiting for transfers between devices, tiled_gather(): return lax.all_to_all(copies, axis, dim, dim, tiled=True)  362 us
    scatter-add x1, other arithmetic, per_device(): jax.ops.segment_sum(products, tile_pairs[:, 0], num_segments=row_blocks)  69.8 us
    select_n x1, local copies, waits for them, and re-layouts, per_device(): products = jnp.where(alive[:, None, None], products, 0.0)  33.4 us
    dot_general x1, matrix products, per_device(): jnp.einsum('tij,tjd->tid', tile_block, chosen, preferred_element_type=jnp...  22.5 us
    all_to_all x1, waiting for transfers between devices, per_device(): lax.all_to_all(sectioned, 'tm', split_axis=1, concat_axis=0, tiled=True)  15.8 us
    gather x1, local copies, waits for them, and re-layouts, per_device(): chosen = blocks[tile_pairs[:, 1]]  14.1 us
  transfers between devices with their start and end apart: 2, of which 2 were waited for; matrix products, arithmetic and copies ran while one was open for 0% of the time, Pallas kernels for 0%

profile of v1, /device:TPU:1, one launch (start us, length us, event | category | flops | bytes accessed | tf_op | source)
XLA Modules:
  0.0 605.0 jit_solution(6932218908597695649)
XLA Ops:
  0.0 1.4 bitcast_dynamic-update-slice_fusion.14
  1.5 1.3 bitcast_dynamic-update-slice_fusion.13
  2.8 0.1 bitcast_dynamic-update-slice_fusion.12
  2.8 0.1 bitcast_dynamic-update-slice_fusion.11
  2.9 0.1 bitcast_dynamic-update-slice_fusion.10
  3.0 0.1 bitcast_dynamic-update-slice_fusion.9
  3.1 0.1 bitcast_dynamic-update-slice_fusion.8
  3.1 0.1 bitcast_dynamic-update-slice_fusion.7
  3.2 0.1 bitcast_dynamic-update-slice_fusion.6
  3.3 0.1 bitcast_dynamic-update-slice_fusion.5
  3.4 0.1 bitcast_dynamic-update-slice_fusion.4
  3.5 0.1 bitcast_dynamic-update-slice_fusion.3
  3.5 0.1 bitcast_dynamic-update-slice_fusion.2
  3.6 0.1 bitcast_dynamic-update-slice_fusion.1
  3.7 0.1 bitcast_dynamic-update-slice_fusion
  3.8 0.1 bitcast_dynamic-update-slice_fusion.15
  3.9 5.7 copy-done.2
  9.6 10.1 %all-to-all-start = ((bf16[16,1024,512]{2,1,0:T(8,128)(2,1)}), bf16[16,1024,512]{2,1,0:T(8,128)(2,1)}, u32[]{:S(2)}, u32[]{:S(2)}) async-start(bf16[16,1024,512]{2,1,0:T(8,128)(2,1)} %bitcast.72), calls=%async_computation | async-start | bytes 33554432 | tf_op jit(solution)/shard_map/all_to_all | solution.py:12
  20.4 362.4 %all-to-all-done = bf16[16,1024,512]{2,1,0:T(8,128)(2,1)} async-done(((bf16[16,1024,512]{2,1,0:T(8,128)(2,1)}), bf16[16,1024,512]{2,1,0:T(8,128)(2,1)}, u32[]{:S(2)}, u32[]{:S(2)}) %all-to-all-start) | async-done | bytes 16777248 | tf_op jit(solution)/shard_map/all_to_all | solution.py:12
  382.7 14.1 %gather_fusion = bf16[128,128,512]{2,1,0:T(8,128)(2,1)} fusion(bf16[128,128,512]{2,1,0:T(8,128)(2,1)} %bitcast.5, s32[1024]{0:T(1024)S(1)} %pad_clamp_fusion), kind=kCustom, calls=%fused_computation | custom fusion | bytes 33554944 | tf_op jit(solution)/shard_map/gather | solution.py:77
  396.8 22.5 %select_bitcast_fusion = f32[128,128,512]{1,2,0:T(8,128)} fusion(pred[128]{0:T(512)(128)(4,1)S(1)} %iota_compare_fusion.1, bf16[128,128,512]{2,1,0:T(8,128)(2,1)} %gather_fusion, bf16[1,128,128,128]{3,2,1,0:T(8,128)(2,1)} %param.16), kind=kOutput, calls=%fused_computation.3 | convolution fusion | flops 2155872256 | bytes 54526080 | tf_op jit(solution)/shard_map/tij,tjd->tid/dot_general | solution.py:78
  419.3 33.4 %copy.36 = f32[128,128,512]{2,1,0:T(8,128)} copy(f32[128,128,512]{1,2,0:T(8,128)} %select_bitcast_fusion) | data formatting | bytes 67108864 | tf_op jit(solution)/shard_map/jit(_where)/select_n | solution.py:79
  452.7 1.6 broadcast_in_dim.40
  454.3 69.8 %scatter_fusion = f32[8,128,512]{2,1,0:T(8,128)} fusion(f32[8,128,512]{2,1,0:T(8,128)} %broadcast_in_dim.40, s32[128]{0:T(128)S(1)} %get-tuple-element.9, f32[128,128,512]{2,1,0:T(8,128)} %copy.36), kind=kCustom, calls=%fused_computation.1 | custom fusion | flops 8388608 | bytes 100663808 | tf_op jit(solution)/shard_map/scatter-add | solution.py:80
  524.1 1.8 convert_element_type.48
  525.9 0.7 fusion.62
  526.7 0.0 copy-start.4
  526.7 0.0 copy-start.5
  526.7 0.0 copy-start.6
  526.7 2.1 fusion.17
  528.8 7.1 %all-to-all-start.1 = ((bf16[1,16,64,512]{3,2,0,1:T(8,128)(2,1)}), bf16[1,16,64,512]{3,2,0,1:T(8,128)(2,1)S(1)}, u32[]{:S(2)}, u32[]{:S(2)}) async-start(bf16[1,16,64,512]{3,2,0,1:T(8,128)(2,1)} %bitcast.74), calls=%async_computation.1 | async-start | bytes 2097152 | tf_op jit(solution)/shard_map/all_to_all | solution.py:89
  536.0 15.8 %all-to-all-done.1 = bf16[1,16,64,512]{3,2,0,1:T(8,128)(2,1)S(1)} async-done(((bf16[1,16,64,512]{3,2,0,1:T(8,128)(2,1)}), bf16[1,16,64,512]{3,2,0,1:T(8,128)(2,1)S(1)}, u32[]{:S(2)}, u32[]{:S(2)}) %all-to-all-start.1) | async-done | bytes 1048608 | tf_op jit(solution)/shard_map/all_to_all | solution.py:89
  551.8 0.3 fusion.21
  552.2 1.9 convolution_convert_fusion
  554.1 1.8 fusion.60
  555.8 3.9 reshape.57
  559.7 3.9 reshape.58
  563.6 6.7 %fusion.26 = f32[64,8,16,16]{2,3,1,0:T(8,128)} fusion(bf16[16,64,8,64]{3,2,1,0:T(8,128)(2,1)} %reshape.58, bf16[16,64,8,64]{3,2,1,0:T(8,128)(2,1)} %reshape.57), kind=kOutput, calls=%fused_computation.33 | convolution fusion | flops 16777216 | bytes 2621440 | tf_op jit(solution)/shard_map/sihd,tihd->ihst/dot_general | solution.py:33
  570.4 4.7 copy.41
  575.1 2.7 fusion.61
  577.7 0.1 divide_convert_fusion
  577.9 3.9 copy.43
  581.8 3.9 reshape.56
  585.7 3.7 convert_bitcast_fusion
  589.5 1.9 copy.44
  591.3 4.0 reshape.59
  595.4 3.3 multiply_reduce_fusion
  598.7 6.3 %add_convert_fusion = bf16[16,64,512]{2,1,0:T(8,128)(2,1)} fusion(f32[16,64,512]{2,1,0:T(8,128)} %get-tuple-element.13, bf16[1024,512]{1,0:T(8,128)(2,1)} %param.25, bf16[512,1024]{1,0:T(8,128)(2,1)} %param.24, f32[512]{0:T(512)S(1)} %convert_element_type.60, f32[16,64]{1,0:T(8,128)S(1)} %add_rsqrt_fusion), kind=kOutput, calls=%fused_computation.36 | convolution fusion | flops 2159542272 | bytes 5249024 | tf_op jit(solution)/shard_map/sid,de->sie/dot_general | solution.py:21
  (25 shorter events, 0.1 us)
Async XLA Ops:
  0.0 552.2 %copy-start = (bf16[512,1536]{1,0:T(8,128)(2,1)S(1)}, bf16[512,1536]{1,0:T(8,128)(2,1)}, u32[]{:S(2)}) copy-start(bf16[512,1536]{1,0:T(8,128)(2,1)} %param.21) | copy-start | bytes 4718596
  0.0 2.7 copy-start.1
  3.9 5.7 copy-start.2
  9.6 10.8 %copy-start.7 = (s32[1,128,2]{1,2,0:T(2,128)S(1)}, s32[1,128,2]{1,2,0:T(2,128)}, u32[]{:S(2)}) copy-start(s32[1,128,2]{1,2,0:T(2,128)} %param.14) | copy-start | bytes 3076
  9.6 373.2 %all-to-all-start = ((bf16[16,1024,512]{2,1,0:T(8,128)(2,1)}), bf16[16,1024,512]{2,1,0:T(8,128)(2,1)}, u32[]{:S(2)}, u32[]{:S(2)}) async-start(bf16[16,1024,512]{2,1,0:T(8,128)(2,1)} %bitcast.72), calls=%async_computation | async-start | bytes 33554432 | tf_op jit(solution)/shard_map/all_to_all | solution.py:12
  454.3 71.6 %copy-start.3 = (bf16[512,512]{1,0:T(8,128)(2,1)S(1)}, bf16[512,512]{1,0:T(8,128)(2,1)}, u32[]{:S(2)}) copy-start(bf16[512,512]{1,0:T(8,128)(2,1)} %param.17) | copy-start | bytes 1572868
  524.1 2.5 copy-start.8
  526.7 9.3 %copy-start.4 = (bf16[16,512]{1,0:T(8,128)(2,1)S(1)}, bf16[16,512]{1,0:T(8,128)(2,1)}, u32[]{:S(2)}) copy-start(bf16[16,512]{1,0:T(8,128)(2,1)} %param.19) | copy-start | bytes 49156
  526.7 9.3 %copy-start.5 = (bf16[512]{0:T(512)(128)(2,1)S(1)}, bf16[512]{0:T(512)(128)(2,1)}, u32[]{:S(2)}) copy-start(bf16[512]{0:T(512)(128)(2,1)} %param.20) | copy-start | bytes 3076
  526.7 9.3 %copy-start.6 = (bf16[512]{0:T(512)(128)(2,1)S(1)}, bf16[512]{0:T(512)(128)(2,1)}, u32[]{:S(2)}) copy-start(bf16[512]{0:T(512)(128)(2,1)} %param.23) | copy-start | bytes 3076
  528.8 23.0 %all-to-all-start.1 = ((bf16[1,16,64,512]{3,2,0,1:T(8,128)(2,1)}), bf16[1,16,64,512]{3,2,0,1:T(8,128)(2,1)S(1)}, u32[]{:S(2)}, u32[]{:S(2)}) async-start(bf16[1,16,64,512]{3,2,0,1:T(8,128)(2,1)} %bitcast.74), calls=%async_computation.1 | async-start | bytes 2097152 | tf_op jit(solution)/shard_map/all_to_all | solution.py:89
  589.4 5.9 copy-start.9
